TPU v7x, 256 devices: a whole 4x4x8 slice. The times are simulated.
256 devices in a mesh: samp: 8 (over x, z_hi), feat: 32 (over y, z_lo, core).
Axes of the slice: x: 4, y: 4, z: 8 (z_hi: 2, z_lo: 4; z = z_hi * 4 + z_lo), core: 2. Of those that a mesh axis runs over, the one named last changes fastest.
Arguments:
- embeddings: bfloat16 [8192, 1024], P('samp'), may hold values from -6 to 6
- frequencies: bfloat16 [1024, 8192], P(None, 'feat'), may hold values from -0.1875 to 0.1875
- phases: float32 [8192], P('feat'), may hold values from -3.140625 to 3.140625
- treat_freq: float32 [8192], P('feat'), may hold values from -3.140625 to 3.140625
- treatment: int32 [8192], P('samp'), may hold values from 0 to 1
- flips: int32 [8192], P('samp'), may hold values from 0 to 1
- panel: int32 [1], replicated, may hold values from 0 to 15
Outputs:
- schur: float32 [8192, 8192], P('samp', 'feat')
- panel_factor: float32 [8192, 512], P('samp')
- moment_scaled: float32 [8192], P('feat')
All inputs are finite; a program needn't handle non-finite values.
Results may differ from a plain program's by a relative error of at most 0.0032.
Values may be sent and summed in bfloat16 or wider, within the bound.
No kernel may reach another device: no remote copies, remote signals or barrier semaphores. Data moves between devices by JAX's collectives and lax.ppermute only.
A program may use at most 128 MiB of HBM per device.

v0:
```python
import jax
import jax.numpy as jnp
from jax import lax
from jax.sharding import PartitionSpec as P

PANEL = 512
ridge = 0.1
root_two = 1.4142135623730951


def broadcast(shard, axis, root):
    mine = lax.axis_index(axis) == root
    return lax.psum(jnp.where(mine, shard, jnp.zeros_like(shard)), axis)


def cosine_map(project, phases, treat_freq, treated):
    return root_two * jnp.cos(project + phases[None, :] + treated[:, None] * treat_freq[None, :])


def inner_rows(left, right):
    return lax.dot_general(
        left, right, (((0,), (0,)), ((), ())), preferred_element_type=jnp.float32
    )


def per_device(embeddings, frequencies, phases, treat_freq, treatment, flips, panel):
    project = jnp.dot(embeddings, frequencies, preferred_element_type=jnp.float32)
    treated = treatment.astype(jnp.float32)
    flipped = flips.astype(jnp.float32)
    counter = treated + flipped - 2.0 * treated * flipped
    observed = cosine_map(project, phases, treat_freq, treated)
    counterfactual = cosine_map(project, phases, treat_freq, counter)
    feature_obs = observed.astype(jnp.bfloat16)
    samp_size = lax.axis_size("samp")
    feat_size = lax.axis_size("feat")
    sample_count = embeddings.shape[0] * samp_size
    col_width = feature_obs.shape[1]
    feat_total = col_width * feat_size
    row_height = feat_total // samp_size
    samp_index = lax.axis_index("samp")
    feat_index = lax.axis_index("feat")
    moment_part = jnp.sum(counterfactual - observed, axis=0)
    moment_sum = lax.psum(moment_part, "samp") / sample_count
    first_col = panel[0] * PANEL
    panel_devs = PANEL // col_width
    first_dev = first_col // col_width
    gram_part = inner_rows(lax.all_gather(feature_obs, "feat", axis=1, tiled=True), feature_obs)
    gram_raw = lax.psum_scatter(gram_part, "samp", scatter_dimension=0, tiled=True)
    row_ids = samp_index * row_height + lax.broadcasted_iota(jnp.int32, (row_height, col_width), 0)
    col_ids = feat_index * col_width + lax.broadcasted_iota(jnp.int32, (row_height, col_width), 1)
    gram_own = gram_raw / sample_count + ridge * (row_ids == col_ids).astype(jnp.float32)
    col_parts = []
    moment_parts = []
    for member in range(panel_devs):
        got_cols, got_moment = (
            broadcast(gram_own, "feat", first_dev + member),
            broadcast(moment_sum, "feat", first_dev + member),
        )
        col_parts.append(got_cols)
        moment_parts.append(got_moment)
    panel_cols = jnp.concatenate(col_parts, axis=1)
    moment_panel = jnp.concatenate(moment_parts, axis=0)
    source_samp = first_col // row_height
    offset_row = first_col % row_height
    pivot_local = lax.dynamic_slice_in_dim(panel_cols, offset_row, PANEL, 0)
    cross_local = lax.dynamic_slice_in_dim(gram_own, offset_row, PANEL, 0)
    pivot, cross = (
        broadcast(pivot_local, "samp", source_samp),
        broadcast(cross_local, "samp", source_samp),
    )
    lower = jnp.linalg.cholesky(pivot)
    factor_t = lax.linalg.triangular_solve(lower, panel_cols.T, left_side=True, lower=True)
    panel_factor = factor_t.T
    cross_t = lax.linalg.triangular_solve(lower, cross, left_side=True, lower=True)
    schur = gram_own - jnp.dot(panel_factor, cross_t, precision=lax.Precision.HIGHEST)
    solved = lax.linalg.triangular_solve(lower, moment_panel[:, None], left_side=True, lower=True)[
        :, 0
    ]
    reduced = moment_sum - jnp.dot(cross_t.T, solved, precision=lax.Precision.HIGHEST)
    moment_scaled = jnp.sqrt(jnp.float32(sample_count)) * reduced
    return (schur, panel_factor, moment_scaled)


def solution(mesh):
    return jax.shard_map(
        per_device,
        mesh=mesh,
        in_specs=(
            P("samp", None),
            P(None, "feat"),
            P("feat"),
            P("feat"),
            P("samp"),
            P("samp"),
            P(),
        ),
        out_specs=(P("samp", "feat"), P("samp", None), P("feat")),
        check_vma=False,
    )
```

profile of v0, /device:TPU:8, one launch (start us, length us, event | category | flops | bytes accessed | tf_op | source)
XLA Modules:
  0.0 977.7 jit_solution(12588586258870872119)
XLA Ops:
  7.2 0.8 convert_element_type.10
  8.1 0.7 multiply_subtract_fusion
  8.8 9.7 subtract_reduce_fusion
  18.5 127.0 %all-gather.2.cloned.1.call-done = bf16[1024,8192]{1,0:T(8,128)(2,1)} async-done(((bf16[1024,256]{1,0:T(8,128)(2,1)}), bf16[1024,8192]{1,0:T(8,128)(2,1)}) %all-gather.2.cloned.1.call-update) | async-done | bytes 16777232 | tf_op jit(solution)/shard_map/all_gather | solution.py:47
  145.5 13.7 %fusion.87 = f32[8192,256]{0,1:T(8,128)} fusion(bf16[1024,8192]{1,0:T(8,128)(2,1)} %all-gather.2.cloned.1.call-done, bf16[1024,256]{1,0:T(8,128)(2,1)} %get-tuple-element.37), kind=kOutput, calls=%fused_computation.148 | convolution fusion | flops 4294967296 | bytes 25690112 | tf_op jit(solution)/shard_map/dot_general | solution.py:21
  160.0 184.1 %reduce-scatter.2.cloned.1.call-done = f32[1024,256]{0,1:T(8,128)} async-done(((f32[8192,256]{0,1:T(8,128)}), f32[1024,256]{0,1:T(8,128)}) %reduce-scatter.2.cloned.1.call-update) | async-done | bytes 1048592 | tf_op jit(solution)/shard_map/reduce_scatter | solution.py:48
  344.1 2.4 broadcast_select_fusion
  346.6 1.1 broadcast_select_fusion.1
  347.9 1.0 dynamic-slice_select_fusion.1
  348.9 263.1 %all-reduce.7.cloned.1.call-done = (f32[1024,256]{0,1:T(8,128)}, f32[1024,256]{0,1:T(8,128)}) async-done(((f32[1024,256]{0,1:T(8,128)}, f32[1024,256]{0,1:T(8,128)}), (f32[1024,256]{0,1:T(8,128)}, f32[1024,256]{0,1:T(8,128)})) %all-reduce.7.cloned.1.call-update) | async-done | bytes 2097168 | tf_op jit(solution)/shard_map/psum | solution.py:13
  612.0 1.4 constant_dynamic-update-slice_fusion.1
  613.6 1.3 copy-done.1
  614.9 1.3 dynamic-slice_select_fusion
  616.3 29.4 %psum.53 = f32[256]{0:T(256)S(1)} all-reduce(f32[256]{0:T(256)S(1)} %get-tuple-element.36), channel_id=1, replica_groups=mesh['samp'=8,'feat'=32] {'samp'}, use_global_device_ids=true, to_apply=%region_14.15 | all-reduce | flops 256 | bytes 2048 | tf_op jit(solution)/shard_map/psum | solution.py:43
  645.7 73.2 %all-reduce.1 = (f32[256]{0:T(256)S(1)}, f32[256]{0:T(256)S(1)}) all-reduce(f32[256]{0:T(256)S(1)} %get-tuple-element.45, f32[256]{0:T(256)S(1)} %get-tuple-element.44), channel_id=1, replica_groups=mesh['samp'=8,'feat'=32] {'feat'}, use_global_device_ids=true, to_apply=%region_15.16 | all-reduce | flops 512 | bytes 4096 | tf_op jit(solution)/shard_map/psum | solution.py:13
  719.4 72.7 %all-reduce.9.cloned.1.call-done = (f32[512,512]{0,1:T(8,128)}, f32[512,256]{0,1:T(8,128)}) async-done(((f32[512,512]{0,1:T(8,128)}, f32[512,256]{0,1:T(8,128)}), (f32[512,512]{0,1:T(8,128)}, f32[512,256]{0,1:T(8,128)})) %all-reduce.9.cloned.1.call-update) | async-done | bytes 1572880 | tf_op jit(solution)/shard_map/psum | solution.py:13
  792.2 2.6 copy.11
  794.8 1.4 fusion.19
  796.3 1.0 copy-done.7
  797.2 11.7 %cholesky.103 = f32[128,128]{1,0:T(8,128)S(1)} custom-call(f32[128,128]{1,0:T(8,128)S(1)} %cholesky.263), custom_call_target="Cholesky" | custom-call | tf_op jit(solution)/shard_map/jit(cholesky)/cholesky | solution.py:71
  809.0 9.8 %custom-call.34 = f32[1,128,128]{1,2,0:T(8,128)S(1)} custom-call(f32[1,128,128]{2,1,0:T(8,128)S(1)} %get-tuple-element.43), custom_call_target="InvertDiagBlocksLowerTriangular" | custom-call | tf_op jit(solution)/shard_map/jit(cholesky)/cholesky | solution.py:71
  818.8 1.2 fusion.35
  820.0 1.3 convolution_subtract_fusion.3
  821.3 11.7 %cholesky.215 = f32[128,128]{1,0:T(8,128)S(1)} custom-call(f32[128,128]{1,0:T(8,128)S(1)} %cholesky.267), custom_call_target="Cholesky" | custom-call | tf_op jit(solution)/shard_map/jit(cholesky)/cholesky | solution.py:71
  833.6 0.7 copy.14
  834.4 0.7 copy.12
  835.2 10.6 %custom-call.35 = f32[1,128,128]{1,2,0:T(8,128)} custom-call(f32[1,128,128]{2,1,0:T(8,128)S(1)} %get-tuple-element.41), custom_call_target="InvertDiagBlocksLowerTriangular" | custom-call | tf_op jit(solution)/shard_map/jit(cholesky)/cholesky | solution.py:71
  845.7 1.0 cholesky.222
  846.7 0.8 constant_dynamic-update-slice_fusion.3
  847.6 1.2 convolution_dynamic-update-slice_fusion
  848.7 1.5 convolution_subtract_fusion.6
  850.3 11.7 %cholesky.236 = f32[128,128]{1,0:T(8,128)S(1)} custom-call(f32[128,128]{1,0:T(8,128)S(1)} %cholesky.272), custom_call_target="Cholesky" | custom-call | tf_op jit(solution)/shard_map/jit(cholesky)/cholesky | solution.py:71
  862.1 9.8 %custom-call.36 = f32[1,128,128]{1,2,0:T(8,128)S(1)} custom-call(f32[1,128,128]{2,1,0:T(8,128)S(1)} %get-tuple-element.39), custom_call_target="InvertDiagBlocksLowerTriangular" | custom-call | tf_op jit(solution)/shard_map/jit(cholesky)/cholesky | solution.py:71
  872.2 1.3 convolution_subtract_fusion.8
  873.6 11.9 %cholesky.253 = f32[128,128]{1,0:T(8,128)S(1)} custom-call(f32[128,128]{1,0:T(8,128)S(1)} %convolution_subtract_fusion.8), custom_call_target="Cholesky" | custom-call | tf_op jit(solution)/shard_map/jit(cholesky)/cholesky | solution.py:71
  886.2 0.7 compare_reduce_fusion
  886.9 1.3 compare_reduce_fusion.2
  890.7 1.1 select_select_fusion
  891.8 14.1 %while.1 = (s32[]{:T(128)}, f32[512,512]{0,1:T(8,128)}, s32[4,2]{0,1:T(2,128)S(1)}, f32[4,128,128]{2,1,0:T(8,128)}, s32[]{:T(128)}) while((s32[]{:T(128)}, f32[512,512]{0,1:T(8,128)}, s32[4,2]{0,1:T(2,128)S(1)}, f32[4,128,128]{2,1,0:T(8,128)}, s32[]{:T(128)}) %tuple.32), condition=%wide.while_cond, body=%wide.while_body.sunk | while | flops 2 | bytes 393829 | solution.py:72
  892.4 2.2 dynamic-slice.7
  895.9 2.2 dynamic-slice.7
  898.3 0.6 bitcast_dynamic-update-slice_fusion.2
  899.5 2.2 dynamic-slice.7
  903.0 2.2 dynamic-slice.7
  905.3 0.6 bitcast_dynamic-update-slice_fusion.2
  905.9 40.2 %custom-call.37 = f32[4,128,128]{1,2,0:T(8,128)S(1)} custom-call(f32[4,128,128]{2,1,0:T(8,128)} %get-tuple-element.10), custom_call_target="InvertDiagBlocksLowerTriangular" | custom-call | tf_op jit(solution)/shard_map/triangular_solve | solution.py:72
  946.3 1.1 fusion.12
  947.6 1.1 fusion.13
  948.9 1.2 fusion.15
  950.2 1.2 fusion.40
  951.4 1.3 convolution_subtract_fusion.7
  953.1 1.6 convolution_subtract_fusion.5
  955.0 1.7 convolution_subtract_fusion.4
  957.1 0.6 fusion.21
  957.7 0.6 convolution_subtract_fusion.2
  958.4 0.6 fusion.53
  959.0 0.7 convolution_subtract_fusion.1
  959.7 0.6 fusion.55
  960.4 1.1 fusion.6
  961.5 0.6 fusion.57
  962.2 1.6 fusion.9
  963.8 2.0 convolution_subtract_fusion
  966.8 2.9 copy.22
  969.6 1.3 copy.21
  (71 shorter events, 9.6 us)
Async XLA Ops:
  7.2 1.6 copy-start
  7.2 138.3 %all-gather.2.cloned.1.call-start = ((), (), s32[]{:S(2)}) async-start(), calls=%async_computation.1 | async-start | bytes 17301504 | tf_op jit(solution)/shard_map/all_gather | solution.py:47
  18.5 325.7 %reduce-scatter.2.cloned.1.call-start = ((), (), s32[]{:S(2)}) async-start(), calls=%async_computation.2 | async-start | bytes 9437184 | tf_op jit(solution)/shard_map/reduce_scatter | solution.py:48
  159.2 452.7 %all-reduce.7.cloned.1.call-start = ((), (), s32[]{:S(2)}) async-start(), calls=%async_computation.3 | async-start | bytes 4194304 | tf_op jit(solution)/shard_map/psum | solution.py:13
  346.6 1.3 copy-start.3
  347.7 444.5 %all-reduce.9.cloned.1.call-start = ((), (), s32[]{:S(2)}) async-start(), calls=%async_computation.4 | async-start | bytes 3145728 | tf_op jit(solution)/shard_map/psum | solution.py:13
  612.0 1.5 copy-start.8
  613.6 1.3 copy-start.1
  792.2 2.6 copy-start.6
  796.3 1.0 copy-start.7
  848.7 43.0 %copy-start.9 = (s32[4]{0:T(128)S(1)}, s32[4]{0:T(128)}, u32[]{:S(2)}) copy-start(s32[4]{0:T(128)} %iota_multiply_fusion) | copy-start | bytes 52
  905.9 49.1 %copy-start.5 = (f32[512,512]{0,1:T(8,128)S(1)}, f32[512,512]{0,1:T(8,128)}, u32[]{:S(2)}) copy-start(f32[512,512]{0,1:T(8,128)} %get-tuple-element.104) | copy-start | bytes 3145732
  946.1 10.9 %copy-start.2 = (f32[1024,512]{0,1:T(8,128)S(1)}, f32[1024,512]{0,1:T(8,128)}, u32[]{:S(2)}) copy-start(f32[1024,512]{0,1:T(8,128)} %copy-done.1) | copy-start | bytes 6291460
  962.1 1.6 copy-start.4
Sparse Core Ops, SparseCore 0:
  18.6 126.8 all-gather.1
  159.4 184.7 reduce-scatter.1
  347.8 264.0 all-reduce.6
  616.4 175.7 all-reduce.8
where the time goes:
time: 985 us; the launch traced here: 978 us
  waiting for transfers between devices  647 us (66%)
  other arithmetic  133 us (14%)
  blocking collectives  103 us (10%)
  matrix products  48.4 us (5%)
  local copies, waits for them, and re-layouts  28.5 us (3%)
  between operations  17.5 us (2%)
    psum x2, waiting for transfers between devices, broadcast(): return lax.psum(jnp.where(mine, shard, jnp.zeros_like(shard)), axis)  336 us
    reduce_scatter x1, waiting for transfers between devices, per_device(): lax.psum_scatter(gram_part, 'samp', scatter_dimension=0, tiled=True)  184 us
    all_gather x1, waiting for transfers between devices, per_device(): lax.all_gather(feature_obs, 'feat', axis=1, tiled=True)  127 us
    another operation x14, other arithmetic, per_device(): lower = jnp.linalg.cholesky(pivot)  80.5 us
    psum x1, blocking collectives, broadcast(): return lax.psum(jnp.where(mine, shard, jnp.zeros_like(shard)), axis)  73.2 us
    another operation x3, other arithmetic, per_device(): lax.linalg.triangular_solve(lower, panel_cols.T, left_side=True, lower=True)  41.9 us
    psum x1, blocking collectives, per_device(): moment_sum = lax.psum(moment_part, 'samp') / sample_count  29.4 us
  transfers between devices with their start and end apart: 4, of which 4 were waited for; matrix products, arithmetic and copies ran while one was open for 0% of the time, Pallas kernels for 0%

commit v1 on v0

--- a/solution.py
+++ b/solution.py
@@ -10,7 +10,7 @@
 
 def broadcast(shard, axis, root):
     mine = lax.axis_index(axis) == root
-    return lax.psum(jnp.where(mine, shard, jnp.zeros_like(shard)), axis)
+    return jnp.sum(lax.all_gather(jnp.where(mine, shard, jnp.zeros_like(shard)), axis), axis=0)
 
 
 def cosine_map(project, phases, treat_freq, treated):

time: 985 us -> 1190 us (1.21)
  waiting for transfers between devices: 647 us -> 816 us
  other arithmetic: 133 us -> 173 us
  local copies, waits for them, and re-layouts: 28.5 us -> 14.8 us
    all_gather x0 -> x4, waiting for transfers between devices: none -> 504 us  [broadcast(): lax.all_gather(jnp.where(mine, shard, jnp.zeros_like(shard)), axis)]
    psum x2 -> x0, waiting for transfers between devices: 336 us -> none  [broadcast(): return lax.psum(jnp.where(mine, shard, jnp.zeros_like(shard)), axis)]
    all_gather x0 -> x2, blocking collectives: none -> 77.4 us  [broadcast(): lax.all_gather(jnp.where(mine, shard, jnp.zeros_like(shard)), axis)]
    psum x1 -> x0, blocking collectives: 73.2 us -> none  [broadcast(): return lax.psum(jnp.where(mine, shard, jnp.zeros_like(shard)), axis)]
    reduce_sum x0 -> x6, other arithmetic: none -> 31.8 us  [broadcast(): jnp.sum(lax.all_gather(jnp.where(mine, shard, jnp.zeros_like(shard)), axi...]
  transfers between devices with their start and end apart: 4 -> 6, of which waited for: 4 -> 5; matrix products, arithmetic and copies ran while one was open for 0% -> 3% of each run, Pallas kernels for 0% -> 0%
where the time goes in v1:
time: 1190 us; the launch traced here: 1180 us
  waiting for transfers between devices  816 us (69%)
  other arithmetic  173 us (15%)
  blocking collectives  113 us (9%)
  matrix products  48.4 us (4%)
  between operations  18.1 us (2%)
  local copies, waits for them, and re-layouts  14.8 us (1%)
    all_gather x4, waiting for transfers between devices, broadcast(): lax.all_gather(jnp.where(mine, shard, jnp.zeros_like(shard)), axis)  504 us
    reduce_scatter x1, waiting for transfers between devices, per_device(): lax.psum_scatter(gram_part, 'samp', scatter_dimension=0, tiled=True)  184 us
    all_gather x1, waiting for transfers between devices, per_device(): lax.all_gather(feature_obs, 'feat', axis=1, tiled=True)  127 us
    another operation x14, other arithmetic, per_device(): lower = jnp.linalg.cholesky(pivot)  89.9 us
    all_gather x2, blocking collectives, broadcast(): lax.all_gather(jnp.where(mine, shard, jnp.zeros_like(shard)), axis)  77.4 us
    another operation x3, other arithmetic, per_device(): lax.linalg.triangular_solve(lower, panel_cols.T, left_side=True, lower=True)  40.5 us
    psum x1, blocking collectives, per_device(): moment_sum = lax.psum(moment_part, 'samp') / sample_count  35.5 us
    reduce_sum x6, other arithmetic, broadcast(): jnp.sum(lax.all_gather(jnp.where(mine, shard, jnp.zeros_like(shard)), axi...  31.8 us
  transfers between devices with their start and end apart: 6, of which 5 were waited for; matrix products, arithmetic and copies ran while one was open for 3% of the time, Pallas kernels for 0%

profile of v1, /device:TPU:8, one launch (start us, length us, event | category | flops | bytes accessed | tf_op | source)
XLA Modules:
  0.0 1183.2 jit_solution(3955284008430421817)
XLA Ops:
  7.2 0.8 convert_element_type.10
  8.1 0.7 multiply_subtract_fusion
  8.8 9.7 subtract_reduce_fusion
  18.5 127.0 %all-gather.14.cloned.1.call-done = bf16[1024,8192]{1,0:T(8,128)(2,1)} async-done(((bf16[1024,256]{1,0:T(8,128)(2,1)}), bf16[1024,8192]{1,0:T(8,128)(2,1)}) %all-gather.14.cloned.1.call-update) | async-done | bytes 16777232 | tf_op jit(solution)/shard_map/all_gather | solution.py:47
  145.5 13.8 %fusion.90 = f32[8192,256]{1,0:T(8,128)} fusion(bf16[1024,8192]{1,0:T(8,128)(2,1)} %all-gather.14.cloned.1.call-done, bf16[1024,256]{1,0:T(8,128)(2,1)} %get-tuple-element.30), kind=kOutput, calls=%fused_computation.151 | convolution fusion | flops 4294967296 | bytes 25690112 | tf_op jit(solution)/shard_map/dot_general | solution.py:21
  160.1 184.1 %reduce-scatter.2.cloned.1.call-done = f32[1024,256]{1,0:T(8,128)} async-done(((f32[8192,256]{1,0:T(8,128)}), f32[1024,256]{1,0:T(8,128)}) %reduce-scatter.2.cloned.1.call-update) | async-done | bytes 1048592 | tf_op jit(solution)/shard_map/reduce_scatter | solution.py:48
  344.2 2.4 broadcast_select_fusion.1
  346.6 1.0 broadcast_select_fusion
  347.7 0.5 all-gather.16.cloned.1.call-update
  348.3 0.8 dynamic-slice_select_fusion
  349.2 177.1 %all-gather.18.cloned.1.call-done = f32[32768,256]{1,0:T(8,128)} async-done(((f32[1024,256]{1,0:T(8,128)}), f32[32768,256]{1,0:T(8,128)}) %all-gather.18.cloned.1.call-update) | async-done | bytes 33554448 | tf_op jit(solution)/shard_map/all_gather | solution.py:13
  526.3 11.9 %reduce_sum.64 = f32[1024,256]{1,0:T(8,128)S(1)} reduce(f32[32,1024,256]{2,1,0:T(8,128)} %bitcast.125, f32[]{:T(128)} %constant.208.clone.1), dimensions={0}, to_apply=%region_2.3 | reduce | flops 8126464 | bytes 34603012 | tf_op jit(solution)/shard_map/reduce_sum | solution.py:13
  538.3 175.3 %all-gather.16.cloned.1.call-done = f32[32768,256]{1,0:T(8,128)} async-done(((f32[1024,256]{1,0:T(8,128)}), f32[32768,256]{1,0:T(8,128)}) %all-gather.16.cloned.1.call-update) | async-done | bytes 33554448 | tf_op jit(solution)/shard_map/all_gather | solution.py:13
  713.6 11.9 %reduce_sum.63 = f32[1024,256]{1,0:T(8,128)S(1)} reduce(f32[32,1024,256]{2,1,0:T(8,128)} %bitcast.126, f32[]{:T(128)} %constant.208.clone.1), dimensions={0}, to_apply=%region_1.0 | reduce | flops 8126464 | bytes 34603012 | tf_op jit(solution)/shard_map/reduce_sum | solution.py:13
  725.5 1.1 fusion.18
  726.7 35.5 %psum.7 = f32[256]{0:T(256)S(1)} all-reduce(f32[256]{0:T(256)S(1)} %get-tuple-element.29), channel_id=1, replica_groups=mesh['samp'=8,'feat'=32] {'samp'}, use_global_device_ids=true, to_apply=%region_14.15 | all-reduce | flops 256 | bytes 2048 | tf_op jit(solution)/shard_map/psum | solution.py:43
  762.2 40.9 %all-gather.6 = f32[32,1,256]{2,1,0:T(1,128)S(1)} all-gather(f32[1,1,256]{2,1,0:T(1,128)S(1)} %bitcast.130), channel_id=6, replica_groups=mesh['samp'=8,'feat'=32] {'feat'}, dimensions={0}, use_global_device_ids=true | all-gather | bytes 33792 | tf_op jit(solution)/shard_map/all_gather | solution.py:13
  803.2 36.4 %all-gather.7 = f32[32,1,256]{2,1,0:T(1,128)S(1)} all-gather(f32[1,1,256]{2,1,0:T(1,128)S(1)} %bitcast.129), channel_id=7, replica_groups=mesh['samp'=8,'feat'=32] {'feat'}, dimensions={0}, use_global_device_ids=true | all-gather | bytes 33792 | tf_op jit(solution)/shard_map/all_gather | solution.py:13
  839.7 3.4 reduce_sum.66
  843.1 1.6 fusion
  844.7 151.4 %all-gather.20.cloned.1.call-done = f32[4096,512]{1,0:T(8,128)} async-done(((f32[512,512]{1,0:T(8,128)}), f32[4096,512]{1,0:T(8,128)}) %all-gather.20.cloned.1.call-update) | async-done | bytes 8388624 | tf_op jit(solution)/shard_map/all_gather | solution.py:13
  996.1 4.5 reduce_sum.65
  1000.6 0.3 copy.12
  1001.2 1.0 copy-done.3
  1002.2 11.7 cholesky.103
  1014.1 9.8 custom-call.34
  1023.9 1.2 constant_dynamic-update-slice_fusion
  1025.1 1.3 convolution_subtract_fusion.3
  1026.4 23.2 %cholesky.215 = f32[128,128]{1,0:T(8,128)S(1)} custom-call(f32[128,128]{1,0:T(8,128)S(1)} %cholesky.267), custom_call_target="Cholesky" | custom-call | tf_op jit(solution)/shard_map/jit(cholesky)/cholesky | solution.py:71
  1049.6 9.8 custom-call.35
  1059.7 1.3 convolution_subtract_fusion.6
  1061.0 11.7 cholesky.236
  1072.8 0.7 compare_reduce_fusion.1
  1073.5 9.8 custom-call.36
  1083.5 1.2 convolution_subtract_fusion.8
  1084.7 11.7 cholesky.253
  1096.5 0.6 compare_reduce_fusion
  1097.1 0.6 compare_reduce_fusion.2
  1100.5 10.4 while.1
  1100.6 0.5 fusion.109
  1101.1 2.0 bitcast_dynamic-update-slice_fusion.2
  1103.2 0.5 fusion.109
  1103.7 2.0 bitcast_dynamic-update-slice_fusion.2
  1105.8 0.5 fusion.109
  1106.3 2.0 bitcast_dynamic-update-slice_fusion.2
  1108.4 0.5 fusion.109
  1108.9 2.0 bitcast_dynamic-update-slice_fusion.2
  1110.9 40.3 %custom-call.37 = f32[4,128,128]{1,2,0:T(8,128)S(1)} custom-call(f32[4,128,128]{2,1,0:T(8,128)} %get-tuple-element.10), custom_call_target="InvertDiagBlocksLowerTriangular" | custom-call | tf_op jit(solution)/shard_map/triangular_solve | solution.py:72
  1152.7 1.2 fusion.43
  1153.9 1.3 convolution_subtract_fusion.7
  1155.8 0.3 fusion.57
  1156.2 0.4 convolution_subtract_fusion.4
  1156.9 1.7 fusion.24
  1158.6 1.0 convolution_subtract_fusion.2
  1159.6 0.6 fusion.56
  1160.2 1.8 convolution_subtract_fusion.1
  1162.0 0.6 fusion.58
  1162.7 2.7 fusion.7
  1165.4 0.6 fusion.60
  1166.1 1.6 fusion.10
  1167.7 4.5 convolution_subtract_fusion
  1172.1 0.3 fusion.26
  1172.4 0.6 subtract_multiply_fusion
  1173.1 2.9 copy.13
  (55 shorter events, 4.2 us)
Async XLA Ops:
  7.2 1.6 copy-start
  7.2 138.3 %all-gather.14.cloned.1.call-start = ((), (), s32[]{:S(2)}) async-start(), calls=%async_computation.1 | async-start | bytes 17301504 | tf_op jit(solution)/shard_map/all_gather | solution.py:47
  18.5 325.7 %reduce-scatter.2.cloned.1.call-start = ((), (), s32[]{:S(2)}) async-start(), calls=%async_computation.2 | async-start | bytes 9437184 | tf_op jit(solution)/shard_map/reduce_scatter | solution.py:48
  159.3 367.0 %all-gather.18.cloned.1.call-start = ((), (), s32[]{:S(2)}) async-start(), calls=%async_computation.4 | async-start | bytes 34603008 | tf_op jit(solution)/shard_map/all_gather | solution.py:13
  347.6 366.0 %all-gather.16.cloned.1.call-start = ((), (), s32[]{:S(2)}) async-start(), calls=%async_computation.3 | async-start | bytes 34603008 | tf_op jit(solution)/shard_map/all_gather | solution.py:13
  348.2 491.5 %all-gather.22.cloned.1.call-start = ((), (), s32[]{:S(2)}) async-start(), calls=%async_computation.6 | async-start | bytes 4718592 | tf_op jit(solution)/shard_map/all_gather | solution.py:13
  349.2 646.9 %all-gather.20.cloned.1.call-start = ((), (), s32[]{:S(2)}) async-start(), calls=%async_computation.5 | async-start | bytes 9437184 | tf_op jit(solution)/shard_map/all_gather | solution.py:13
  1001.2 1.0 copy-start.3
  1100.5 55.1 %copy-start.4 = (f32[512,256]{1,0:T(8,128)S(1)}, f32[512,256]{1,0:T(8,128)}, u32[]{:S(2)}) copy-start(f32[512,256]{1,0:T(8,128)} %reduce_sum.66) | copy-start | bytes 1572868
  1153.9 4.7 copy-start.2
  1172.4 3.6 copy-start.1
Sparse Core Ops, SparseCore 0:
  18.6 126.8 all-gather.13
  159.4 184.6 reduce-scatter.1
  347.8 178.5 all-gather.17
  528.6 184.9 all-gather.15
  716.1 108.9 all-gather.21
  828.1 167.9 all-gather.19
